TPU v7x, 128 devices: a whole 4x4x4 slice. The times are simulated.
128 devices in a mesh: blk: 8 (over x, y_lo), elem: 16 (over y_hi, z, core).
Axes of the slice: x: 4, y: 4 (y_hi: 2, y_lo: 2; y = y_hi * 2 + y_lo), z: 4, core: 2. Of those that a mesh axis runs over, the one named last changes fastest.
Arguments:
- state: float32 [512, 125, 32, 128], P('blk', None, 'elem'), may hold values from -18 to 18
- rhs: float32 [512, 125, 32, 128], P('blk', None, 'elem'), may hold values from -6 to 6
- to_modal: float32 [125, 125], replicated, may hold values from -1 to 2
- viscous_op: float32 [125, 125], replicated, may hold values from -0.5 to 0.5
- sweep_gain: float32 [512, 125, 125], P('blk'), may hold values from -1 to 1.2
- inv_blocks: float32 [512, 125, 125], P('blk'), may hold values from -0.125 to 0.125
Outputs:
- line_solution: float32 [512, 125, 32, 128], P(('blk', 'elem'))
All inputs are finite; a program needn't handle non-finite values.
Results may differ from a plain program's by a relative error of at most 0.0003.
Values sent between devices are 32-bit elements; how exact they have to be, the bound alone decides.
A program may use at most 128 MiB of HBM per device.

v0:
```python
import jax
import jax.numpy as jnp
from jax import lax
from jax.sharding import PartitionSpec as P

ORDER = 4
NODES = 125


def padded(cells, sides, width, closed):
    for axis, dim in sides:
        count = lax.axis_size(axis)
        ends = count if closed else count - 1
        head = lax.slice_in_dim(cells, 0, width, axis=dim)
        tail = lax.slice_in_dim(cells, cells.shape[dim] - width, cells.shape[dim], axis=dim)
        cells = jnp.concatenate(
            [
                lax.ppermute(tail, axis, [(i, (i + 1) % count) for i in range(ends)]),
                cells,
                lax.ppermute(head, axis, [((i + 1) % count, i) for i in range(ends)]),
            ],
            axis=dim,
        )
    return cells


def shifted(array, axis, by):
    length = lax.axis_size(axis)
    return lax.ppermute(array, axis, [(i, (i + by) % length) for i in range(length)])


def apply_block(matrix, field):
    return jnp.einsum("mn,nja->mja", matrix, field, precision=lax.Precision.HIGHEST)


def body(state, rhs, to_modal, viscous_op, sweep_gain, inv_blocks):
    highest = lax.Precision.HIGHEST
    modal = jnp.einsum("mn,knja->kmja", to_modal, state, precision=highest)
    squares = modal * modal
    upper = jnp.sum(squares[:, ORDER**3 :], axis=1) / NODES
    energy = jnp.mean(squares, axis=1) + 1e-06
    sensor = upper / energy
    beside_all = padded(sensor, (("blk", 0),), 1, True)
    outward = padded(sensor, (("elem", 1),), 1, False)
    smooth = (
        4.0 * sensor + beside_all[2:] + beside_all[:-2] + outward[:, 2:] + outward[:, :-2]
    ) / 8.0
    viscous = jnp.einsum("mn,knja->kmja", viscous_op, state, precision=highest)
    force = rhs + smooth[:, None] * viscous
    coupled = jnp.einsum("kmn,knja->kmja", inv_blocks, force, precision=highest)
    nodes_count = sweep_gain.shape[1]
    identity = jnp.eye(nodes_count, dtype=jnp.float32)
    zero_field = jnp.zeros(coupled.shape[1:], jnp.float32)

    def local_step(carry, inputs):
        product, partial_value = carry
        matrix, source = inputs
        product = jnp.dot(matrix, product, precision=highest)
        partial_value = apply_block(matrix, partial_value) + source
        return ((product, partial_value), (product, partial_value))

    (group_map, group_shift), (prefix_maps, partials) = lax.scan(
        local_step, (identity, zero_field), (sweep_gain, coupled)
    )
    group = lax.axis_index("blk")
    groups = lax.axis_size("blk")

    def cycle_step(turn, carry):
        outgoing, incoming = carry
        received = shifted(outgoing, "blk", 1)
        first_turn = turn == group
        second_turn = turn == groups + group
        pushed = apply_block(group_map, received) + group_shift
        incoming = jnp.where(second_turn, received, incoming)
        outgoing = jnp.where(first_turn | second_turn, pushed, outgoing)
        return (outgoing, incoming)

    _, incoming = lax.fori_loop(0, 2 * groups, cycle_step, (zero_field, zero_field))

    def final_step(field, inputs):
        matrix, source = inputs
        field = apply_block(matrix, field) + source
        return (field, field)

    _, solved = lax.scan(final_step, incoming, (sweep_gain, coupled))
    return lax.all_to_all(solved, "elem", split_axis=0, concat_axis=2, tiled=True)


def solution(mesh):
    in_specs = (
        P("blk", None, "elem", None),
        P("blk", None, "elem", None),
        P(),
        P(),
        P("blk", None, None),
        P("blk", None, None),
    )
    out_specs = P(("blk", "elem"), None, None, None)
    return jax.shard_map(body, mesh=mesh, in_specs=in_specs, out_specs=out_specs, check_vma=False)
```

profile of v0, /device:TPU:1, one launch (start us, length us, event | category | flops | bytes accessed | tf_op | source)
XLA Modules:
  0.0 593.6 jit_solution(11963656463206898649)
XLA Ops:
  0.8 13.6 %fusion.40 = (f32[64,2,128]{2,1,0:T(2,128)S(1)}, f32[64,125,2,128]{3,1,2,0:T(8,128)S(1)}) fusion(f32[125,125]{1,0:T(8,128)S(1)} %copy-done, f32[64,125,2,128]{3,2,1,0:T(2,128)} %param.12), kind=kOutput, calls=%fused_computation.50 | convolution fusion | flops 3076079616 | bytes 16512036 | tf_op jit(solution)/shard_map/mn,knja->kmja/dot_general | solution.py:38
  15.3 3.3 collective-permute-start.3
  18.6 3.5 collective-permute-start.4
  22.2 3.6 collective-permute-start.1
  25.8 10.1 %fusion.18 = f32[64,2,128,125]{2,3,1,0:T(8,128)} fusion(f32[64,125,2,128]{3,2,1,0:T(2,128)S(1)} %copy-done.2, f32[125,125]{1,0:T(8,128)S(1)} %copy-done.4), kind=kOutput, calls=%fused_computation.27 | convolution fusion | flops 3072000000 | bytes 16446500 | tf_op jit(solution)/shard_map/mn,knja->kmja/dot_general | solution.py:48
  35.9 6.5 %copy.18 = f32[64,125,125]{2,1,0:T(8,128)} copy(f32[64,125,125]{2,0,1:T(8,128)} %param.16) | data formatting | bytes 8000000
  42.6 14.6 %bitcast_add_fusion = f32[64,125,2,128]{3,2,1,0:T(2,128)S(1)} fusion(f32[64,125,2,128]{3,2,1,0:T(2,128)} %param.13, f32[64,2,128,125]{2,3,1,0:T(8,128)} %fusion.18, f32[64,2,128]{2,1,0:T(2,128)S(1)} %fusion.31), kind=kLoop, calls=%fused_computation.25 | loop fusion | flops 4096000 | bytes 24641536 | tf_op jit(solution)/shard_map/add | solution.py:49
  57.3 19.4 %fusion.23 = f32[64,125,2,128]{1,3,2,0:T(8,128)} fusion(f32[64,125,125,1]{2,0,1,3:T(8,128)S(1)} %bitcast.66, f32[64,125,2,128]{3,2,1,0:T(2,128)S(1)} %bitcast_add_fusion), kind=kOutput, calls=%fused_computation.33 | convolution fusion | flops 3072000000 | bytes 20384000 | tf_op jit(solution)/shard_map/kmn,knja->kmja/dot_general | solution.py:50
  76.6 9.2 %copy.19 = f32[64,125,2,128]{3,1,2,0:T(8,128)} copy(f32[64,125,2,128]{1,3,2,0:T(8,128)} %fusion.23) | data formatting | bytes 16384000
  85.8 148.7 %while.43 = (s32[]{:T(128)}, f32[125,125]{1,0:T(8,128)S(1)}, f32[125,2,128]{2,0,1:T(8,128)S(1)}, f32[64,125,125]{2,1,0:T(8,128)}, f32[64,125,2,128]{3,1,2,0:T(8,128)}, /*index=5*/s32[]{:T(128)}, s32[]{:T(128)}) while((s32[]{:T(128)}, f32[125,125]{1,0:T(8,128)S(1)}, f32[125,2,128]{2,0,1:T(8,128)S(1)}, f32[64,125,125]{2,1,0:T(8,128)}, ...), condition=%wide.region_3.4_spmd.clone, body=%wide.region_2.3_spmd.clone.sunk | while | flops 71501504 | bytes 1025767 | solution.py:62
  88.2 1.2 convolution_add_fusion.6
  90.5 1.2 convolution_add_fusion.6
  95.1 1.2 convolution_add_fusion.6
  109.1 1.2 convolution_add_fusion.6
  113.7 1.2 convolution_add_fusion.6
  118.4 1.2 convolution_add_fusion.6
  123.0 1.2 convolution_add_fusion.6
  127.7 1.2 convolution_add_fusion.6
  132.3 1.2 convolution_add_fusion.6
  137.0 1.2 convolution_add_fusion.6
  141.6 1.2 convolution_add_fusion.6
  146.3 1.2 convolution_add_fusion.6
  150.9 1.2 convolution_add_fusion.6
  155.6 1.2 convolution_add_fusion.6
  160.2 1.2 convolution_add_fusion.6
  164.9 1.2 convolution_add_fusion.6
  169.5 1.2 convolution_add_fusion.6
  174.1 1.2 convolution_add_fusion.6
  234.6 109.0 %while.44 = (s32[]{:T(128)}, f32[125,2,128]{2,0,1:T(8,128)S(1)}, f32[125,2,128]{2,0,1:T(8,128)S(1)}, s32[]{:T(128)}, s32[]{:T(128)}, /*index=5*/f32[125,125]{1,0...) while((s32[]{:T(128)}, f32[125,2,128]{2,0,1:T(8,128)S(1)}, ...), condition=%wide.region_5.6_spmd.clone, body=%wide.region_4.5_spmd.clone.sunk | while | flops 48160004 | bytes 1726667 | solution.py:78
  234.8 6.9 %collective-permute-done = f32[125,2,128]{2,0,1:T(8,128)S(1)} collective-permute-done((f32[125,2,128]{2,0,1:T(8,128)S(1)}, f32[125,2,128]{2,0,1:T(8,128)S(1)}, u32[]{:S(2)}, u32[]{:S(2)}) %collective-permute-start) | collective-permute-done | bytes 128032 | tf_op jit(solution)/shard_map/while/body/eval_jaxpr/ppermute | solution.py:29
  242.2 6.7 %collective-permute-done = f32[125,2,128]{2,0,1:T(8,128)S(1)} collective-permute-done((f32[125,2,128]{2,0,1:T(8,128)S(1)}, f32[125,2,128]{2,0,1:T(8,128)S(1)}, u32[]{:S(2)}, u32[]{:S(2)}) %collective-permute-start) | collective-permute-done | bytes 128032 | tf_op jit(solution)/shard_map/while/body/eval_jaxpr/ppermute | solution.py:29
  249.4 5.9 collective-permute-done
  255.8 5.9 collective-permute-done
  262.1 5.9 collective-permute-done
  268.5 5.9 collective-permute-done
  274.8 6.1 %collective-permute-done = f32[125,2,128]{2,0,1:T(8,128)S(1)} collective-permute-done((f32[125,2,128]{2,0,1:T(8,128)S(1)}, f32[125,2,128]{2,0,1:T(8,128)S(1)}, u32[]{:S(2)}, u32[]{:S(2)}) %collective-permute-start) | collective-permute-done | bytes 128032 | tf_op jit(solution)/shard_map/while/body/eval_jaxpr/ppermute | solution.py:29
  281.4 7.5 %collective-permute-done = f32[125,2,128]{2,0,1:T(8,128)S(1)} collective-permute-done((f32[125,2,128]{2,0,1:T(8,128)S(1)}, f32[125,2,128]{2,0,1:T(8,128)S(1)}, u32[]{:S(2)}, u32[]{:S(2)}) %collective-permute-start) | collective-permute-done | bytes 128032 | tf_op jit(solution)/shard_map/while/body/eval_jaxpr/ppermute | solution.py:29
  289.3 6.7 %collective-permute-done = f32[125,2,128]{2,0,1:T(8,128)S(1)} collective-permute-done((f32[125,2,128]{2,0,1:T(8,128)S(1)}, f32[125,2,128]{2,0,1:T(8,128)S(1)}, u32[]{:S(2)}, u32[]{:S(2)}) %collective-permute-start) | collective-permute-done | bytes 128032 | tf_op jit(solution)/shard_map/while/body/eval_jaxpr/ppermute | solution.py:29
  296.5 5.9 collective-permute-done
  302.9 5.9 collective-permute-done
  309.2 5.9 collective-permute-done
  315.6 5.9 collective-permute-done
  321.9 6.1 %collective-permute-done = f32[125,2,128]{2,0,1:T(8,128)S(1)} collective-permute-done((f32[125,2,128]{2,0,1:T(8,128)S(1)}, f32[125,2,128]{2,0,1:T(8,128)S(1)}, u32[]{:S(2)}, u32[]{:S(2)}) %collective-permute-start) | collective-permute-done | bytes 128032 | tf_op jit(solution)/shard_map/while/body/eval_jaxpr/ppermute | solution.py:29
  328.5 7.5 %collective-permute-done = f32[125,2,128]{2,0,1:T(8,128)S(1)} collective-permute-done((f32[125,2,128]{2,0,1:T(8,128)S(1)}, f32[125,2,128]{2,0,1:T(8,128)S(1)}, u32[]{:S(2)}, u32[]{:S(2)}) %collective-permute-start) | collective-permute-done | bytes 128032 | tf_op jit(solution)/shard_map/while/body/eval_jaxpr/ppermute | solution.py:29
  336.4 6.7 %collective-permute-done = f32[125,2,128]{2,0,1:T(8,128)S(1)} collective-permute-done((f32[125,2,128]{2,0,1:T(8,128)S(1)}, f32[125,2,128]{2,0,1:T(8,128)S(1)}, u32[]{:S(2)}, u32[]{:S(2)}) %collective-permute-start) | collective-permute-done | bytes 128032 | tf_op jit(solution)/shard_map/while/body/eval_jaxpr/ppermute | solution.py:29
  343.5 127.1 %while.42 = (s32[]{:T(128)}, f32[125,2,128]{2,0,1:T(8,128)S(1)}, f32[64,125,2,128]{3,2,1,0:T(2,128)}, f32[64,125,125]{2,1,0:T(8,128)}, f32[64,125,2,128]{3,1,2,0:T(8,128)}, /*index=5*/s32[]{:T(128)}) while((s32[]{:T(128)}, f32[125,2,128]{2,0,1:T(8,128)S(1)}, f32[64,125,2,128]{3,2,1,0:T(2,128)}, f32[64,125,125]{2,1,0:T(8,128)}, ...), condition=%wide.region_7.8_spmd, body=%wide.region_6.7_spmd.sunk | while | flops 48032000 | bytes 966213 | solution.py:85
  470.6 117.4 %all_to_all.18 = f32[64,125,2,128]{3,2,1,0:T(2,128)S(1)} all-to-all(f32[64,125,2,128]{3,2,1,0:T(2,128)} %get-tuple-element.201), channel_id=1, replica_groups=mesh['blk'=8,'elem'=16] {'elem'}, dimensions={0} | all-to-all | bytes 16384000 | tf_op jit(solution)/shard_map/all_to_all | solution.py:86
  588.0 5.6 copy.23
  (519 shorter events, 258.4 us)
Async XLA Ops:
  0.0 0.8 copy-start
  0.0 25.7 %copy-start.2 = (f32[64,125,2,128]{3,2,1,0:T(2,128)S(1)}, f32[64,125,2,128]{3,2,1,0:T(2,128)}, u32[]{:S(2)}) copy-start(f32[64,125,2,128]{3,2,1,0:T(2,128)} %param.12) | copy-start | bytes 24576004
  0.0 25.7 %copy-start.4 = (f32[125,125]{1,0:T(8,128)S(1)}, f32[125,125]{1,0:T(8,128)}, u32[]{:S(2)}) copy-start(f32[125,125]{1,0:T(8,128)} %param.15) | copy-start | bytes 187504
  15.3 27.1 %collective-permute-start.3 = (f32[64,1,128]{2,1,0:T(1,128)S(1)}, f32[64,1,128]{2,1,0:T(1,128)S(1)}, u32[]{:S(2)}, u32[]{:S(2)}) collective-permute-start(f32[64,1,128]{2,1,0:T(1,128)S(1)} %get-tuple-element.300), channel_id=1, source_target_pairs={{1,0},{2,1},{3,2},{4,3},{5,4},{6,5},{7,6},{8,7},{9,8},{10,9},{11,1... | collective-permute-start | bytes 98312 | tf_op jit(solution)/shard_map/ppermute | solution.py:20
  18.6 23.8 %collective-permute-start.4 = (f32[64,1,128]{2,1,0:T(1,128)S(1)}, f32[64,1,128]{2,1,0:T(1,128)S(1)}, u32[]{:S(2)}, u32[]{:S(2)}) collective-permute-start(f32[64,1,128]{2,1,0:T(1,128)S(1)} %get-tuple-element.301), channel_id=1, source_target_pairs={{0,1},{1,2},{2,3},{3,4},{4,5},{5,6},{6,7},{7,8},{8,9},{9,10},{10,1... | collective-permute-start | bytes 98312 | tf_op jit(solution)/shard_map/ppermute | solution.py:18
  22.2 20.2 %collective-permute-start.1 = (f32[1,2,128]{2,1,0:T(2,128)S(1)}, f32[1,2,128]{2,1,0:T(2,128)S(1)}, u32[]{:S(2)}, u32[]{:S(2)}) collective-permute-start(f32[1,2,128]{2,1,0:T(2,128)S(1)} %get-tuple-element.298), channel_id=1, source_target_pairs={{16,0},{32,16},{48,32},{64,48},{80,64},{96,80},{112,96},{0,112},{1... | collective-permute-start | bytes 3080 | tf_op jit(solution)/shard_map/ppermute | solution.py:20
  25.7 16.7 %collective-permute-start.2 = (f32[1,2,128]{2,1,0:T(2,128)S(1)}, f32[1,2,128]{2,1,0:T(2,128)S(1)}, u32[]{:S(2)}, u32[]{:S(2)}) collective-permute-start(f32[1,2,128]{2,1,0:T(2,128)S(1)} %get-tuple-element.299), channel_id=1, source_target_pairs={{0,16},{16,32},{32,48},{48,64},{64,80},{80,96},{96,112},{112,0},{1... | collective-permute-start | bytes 3080 | tf_op jit(solution)/shard_map/ppermute | solution.py:18
  42.6 14.6 %copy-start.3 = (f32[64,125,125]{2,0,1:T(8,128)S(1)}, f32[64,125,125]{2,0,1:T(8,128)}, u32[]{:S(2)}) copy-start(f32[64,125,125]{2,0,1:T(8,128)} %param.17) | copy-start | bytes 12000004
  234.6 7.2 %collective-permute-start = (f32[125,2,128]{2,0,1:T(8,128)S(1)}, f32[125,2,128]{2,0,1:T(8,128)S(1)}, u32[]{:S(2)}, u32[]{:S(2)}) collective-permute-start(f32[125,2,128]{2,0,1:T(8,128)S(1)} %broadcast_select_fusion.2), channel_id=1, source_target_pairs={{0,16},{16,32},{32,48},{48,64},{64,80},{80,96},{96,112},{112,0},{1... | collective-permute-start | bytes 384008 | tf_op jit(solution)/shard_map/while/body/eval_jaxpr/ppermute | solution.py:29
  242.1 6.8 %collective-permute-start = (f32[125,2,128]{2,0,1:T(8,128)S(1)}, f32[125,2,128]{2,0,1:T(8,128)S(1)}, u32[]{:S(2)}, u32[]{:S(2)}) collective-permute-start(f32[125,2,128]{2,0,1:T(8,128)S(1)} %broadcast_select_fusion.2), channel_id=1, source_target_pairs={{0,16},{16,32},{32,48},{48,64},{64,80},{80,96},{96,112},{112,0},{1... | collective-permute-start | bytes 384008 | tf_op jit(solution)/shard_map/while/body/eval_jaxpr/ppermute | solution.py:29
  249.3 6.0 %collective-permute-start = (f32[125,2,128]{2,0,1:T(8,128)S(1)}, f32[125,2,128]{2,0,1:T(8,128)S(1)}, u32[]{:S(2)}, u32[]{:S(2)}) collective-permute-start(f32[125,2,128]{2,0,1:T(8,128)S(1)} %broadcast_select_fusion.2), channel_id=1, source_target_pairs={{0,16},{16,32},{32,48},{48,64},{64,80},{80,96},{96,112},{112,0},{1... | collective-permute-start | bytes 384008 | tf_op jit(solution)/shard_map/while/body/eval_jaxpr/ppermute | solution.py:29
  255.7 6.0 %collective-permute-start = (f32[125,2,128]{2,0,1:T(8,128)S(1)}, f32[125,2,128]{2,0,1:T(8,128)S(1)}, u32[]{:S(2)}, u32[]{:S(2)}) collective-permute-start(f32[125,2,128]{2,0,1:T(8,128)S(1)} %broadcast_select_fusion.2), channel_id=1, source_target_pairs={{0,16},{16,32},{32,48},{48,64},{64,80},{80,96},{96,112},{112,0},{1... | collective-permute-start | bytes 384008 | tf_op jit(solution)/shard_map/while/body/eval_jaxpr/ppermute | solution.py:29
  262.0 6.0 %collective-permute-start = (f32[125,2,128]{2,0,1:T(8,128)S(1)}, f32[125,2,128]{2,0,1:T(8,128)S(1)}, u32[]{:S(2)}, u32[]{:S(2)}) collective-permute-start(f32[125,2,128]{2,0,1:T(8,128)S(1)} %broadcast_select_fusion.2), channel_id=1, source_target_pairs={{0,16},{16,32},{32,48},{48,64},{64,80},{80,96},{96,112},{112,0},{1... | collective-permute-start | bytes 384008 | tf_op jit(solution)/shard_map/while/body/eval_jaxpr/ppermute | solution.py:29
  268.4 6.0 %collective-permute-start = (f32[125,2,128]{2,0,1:T(8,128)S(1)}, f32[125,2,128]{2,0,1:T(8,128)S(1)}, u32[]{:S(2)}, u32[]{:S(2)}) collective-permute-start(f32[125,2,128]{2,0,1:T(8,128)S(1)} %broadcast_select_fusion.2), channel_id=1, source_target_pairs={{0,16},{16,32},{32,48},{48,64},{64,80},{80,96},{96,112},{112,0},{1... | collective-permute-start | bytes 384008 | tf_op jit(solution)/shard_map/while/body/eval_jaxpr/ppermute | solution.py:29
  274.7 6.2 %collective-permute-start = (f32[125,2,128]{2,0,1:T(8,128)S(1)}, f32[125,2,128]{2,0,1:T(8,128)S(1)}, u32[]{:S(2)}, u32[]{:S(2)}) collective-permute-start(f32[125,2,128]{2,0,1:T(8,128)S(1)} %broadcast_select_fusion.2), channel_id=1, source_target_pairs={{0,16},{16,32},{32,48},{48,64},{64,80},{80,96},{96,112},{112,0},{1... | collective-permute-start | bytes 384008 | tf_op jit(solution)/shard_map/while/body/eval_jaxpr/ppermute | solution.py:29
  281.3 7.6 %collective-permute-start = (f32[125,2,128]{2,0,1:T(8,128)S(1)}, f32[125,2,128]{2,0,1:T(8,128)S(1)}, u32[]{:S(2)}, u32[]{:S(2)}) collective-permute-start(f32[125,2,128]{2,0,1:T(8,128)S(1)} %broadcast_select_fusion.2), channel_id=1, source_target_pairs={{0,16},{16,32},{32,48},{48,64},{64,80},{80,96},{96,112},{112,0},{1... | collective-permute-start | bytes 384008 | tf_op jit(solution)/shard_map/while/body/eval_jaxpr/ppermute | solution.py:29
  289.3 6.8 %collective-permute-start = (f32[125,2,128]{2,0,1:T(8,128)S(1)}, f32[125,2,128]{2,0,1:T(8,128)S(1)}, u32[]{:S(2)}, u32[]{:S(2)}) collective-permute-start(f32[125,2,128]{2,0,1:T(8,128)S(1)} %broadcast_select_fusion.2), channel_id=1, source_target_pairs={{0,16},{16,32},{32,48},{48,64},{64,80},{80,96},{96,112},{112,0},{1... | collective-permute-start | bytes 384008 | tf_op jit(solution)/shard_map/while/body/eval_jaxpr/ppermute | solution.py:29
  296.4 6.0 %collective-permute-start = (f32[125,2,128]{2,0,1:T(8,128)S(1)}, f32[125,2,128]{2,0,1:T(8,128)S(1)}, u32[]{:S(2)}, u32[]{:S(2)}) collective-permute-start(f32[125,2,128]{2,0,1:T(8,128)S(1)} %broadcast_select_fusion.2), channel_id=1, source_target_pairs={{0,16},{16,32},{32,48},{48,64},{64,80},{80,96},{96,112},{112,0},{1... | collective-permute-start | bytes 384008 | tf_op jit(solution)/shard_map/while/body/eval_jaxpr/ppermute | solution.py:29
  302.8 6.0 %collective-permute-start = (f32[125,2,128]{2,0,1:T(8,128)S(1)}, f32[125,2,128]{2,0,1:T(8,128)S(1)}, u32[]{:S(2)}, u32[]{:S(2)}) collective-permute-start(f32[125,2,128]{2,0,1:T(8,128)S(1)} %broadcast_select_fusion.2), channel_id=1, source_target_pairs={{0,16},{16,32},{32,48},{48,64},{64,80},{80,96},{96,112},{112,0},{1... | collective-permute-start | bytes 384008 | tf_op jit(solution)/shard_map/while/body/eval_jaxpr/ppermute | solution.py:29
  309.1 6.0 %collective-permute-start = (f32[125,2,128]{2,0,1:T(8,128)S(1)}, f32[125,2,128]{2,0,1:T(8,128)S(1)}, u32[]{:S(2)}, u32[]{:S(2)}) collective-permute-start(f32[125,2,128]{2,0,1:T(8,128)S(1)} %broadcast_select_fusion.2), channel_id=1, source_target_pairs={{0,16},{16,32},{32,48},{48,64},{64,80},{80,96},{96,112},{112,0},{1... | collective-permute-start | bytes 384008 | tf_op jit(solution)/shard_map/while/body/eval_jaxpr/ppermute | solution.py:29
  315.5 6.0 %collective-permute-start = (f32[125,2,128]{2,0,1:T(8,128)S(1)}, f32[125,2,128]{2,0,1:T(8,128)S(1)}, u32[]{:S(2)}, u32[]{:S(2)}) collective-permute-start(f32[125,2,128]{2,0,1:T(8,128)S(1)} %broadcast_select_fusion.2), channel_id=1, source_target_pairs={{0,16},{16,32},{32,48},{48,64},{64,80},{80,96},{96,112},{112,0},{1... | collective-permute-start | bytes 384008 | tf_op jit(solution)/shard_map/while/body/eval_jaxpr/ppermute | solution.py:29
  321.8 6.2 %collective-permute-start = (f32[125,2,128]{2,0,1:T(8,128)S(1)}, f32[125,2,128]{2,0,1:T(8,128)S(1)}, u32[]{:S(2)}, u32[]{:S(2)}) collective-permute-start(f32[125,2,128]{2,0,1:T(8,128)S(1)} %broadcast_select_fusion.2), channel_id=1, source_target_pairs={{0,16},{16,32},{32,48},{48,64},{64,80},{80,96},{96,112},{112,0},{1... | collective-permute-start | bytes 384008 | tf_op jit(solution)/shard_map/while/body/eval_jaxpr/ppermute | solution.py:29
  328.4 7.6 %collective-permute-start = (f32[125,2,128]{2,0,1:T(8,128)S(1)}, f32[125,2,128]{2,0,1:T(8,128)S(1)}, u32[]{:S(2)}, u32[]{:S(2)}) collective-permute-start(f32[125,2,128]{2,0,1:T(8,128)S(1)} %broadcast_select_fusion.2), channel_id=1, source_target_pairs={{0,16},{16,32},{32,48},{48,64},{64,80},{80,96},{96,112},{112,0},{1... | collective-permute-start | bytes 384008 | tf_op jit(solution)/shard_map/while/body/eval_jaxpr/ppermute | solution.py:29
  336.4 6.8 %collective-permute-start = (f32[125,2,128]{2,0,1:T(8,128)S(1)}, f32[125,2,128]{2,0,1:T(8,128)S(1)}, u32[]{:S(2)}, u32[]{:S(2)}) collective-permute-start(f32[125,2,128]{2,0,1:T(8,128)S(1)} %broadcast_select_fusion.2), channel_id=1, source_target_pairs={{0,16},{16,32},{32,48},{48,64},{64,80},{80,96},{96,112},{112,0},{1... | collective-permute-start | bytes 384008 | tf_op jit(solution)/shard_map/while/body/eval_jaxpr/ppermute | solution.py:29
  588.0 5.6 copy-start.1
where the time goes:
time: 599 us; the launch traced here: 594 us
  matrix products  269 us (45%)
  blocking collectives  117 us (20%)
  waiting for transfers between devices  102 us (17%)
  local copies, waits for them, and re-layouts  72.3 us (12%)
  other arithmetic  16.4 us (3%)
  starting transfers between devices  11.8 us (2%)
    dot_general x144, matrix products, apply_block(): jnp.einsum('mn,nja->mja', matrix, field, precision=lax.Precision.HIGHEST)  159 us
    all_to_all x1, blocking collectives, body(): lax.all_to_all(solved, 'elem', split_axis=0, concat_axis=2, tiled=True)  117 us
    ppermute x16, waiting for transfers between devices, shifted(): lax.ppermute(array, axis, [(i, (i + by) % length) for i in range(length)])  102 us
    dot_general x64, matrix products, local_step(): product = jnp.dot(matrix, product, precision=highest)  67.1 us
    dynamic_update_slice x64, local copies, waits for them, and re-layouts, body(): _, solved = lax.scan(final_step, incoming, (sweep_gain, coupled))  48.4 us
    dot_general x1, matrix products, body(): coupled = jnp.einsum('kmn,knja->kmja', inv_blocks, force, precision=highest)  19.4 us
    unnamed x12, local copies, waits for them, and re-layouts  16.5 us
    add x1, other arithmetic, body(): force = rhs + smooth[:, None] * viscous  14.6 us
  transfers between devices with their start and end apart: 20, of which 16 were waited for; matrix products, arithmetic and copies ran while one was open for 3% of the time, Pallas kernels for 0%

commit v1 on v0

v1 whole, which is shorter than its diff:
```python
import functools

import jax
import jax.numpy as jnp
from jax import lax
from jax.experimental import pallas as pl
from jax.experimental.pallas import tpu as pltpu
from jax.sharding import PartitionSpec as P

ORDER = 4
NODES = 125
LOCAL = 64
CHUNK = 4
PAD = 128
MESH = pl.DeviceIdType.MESH
F32 = jnp.float32
BF16 = jnp.bfloat16


def halves(x):
    high = x.astype(BF16)
    return high, (x - high.astype(F32)).astype(BF16)


def as_rows(x):
    high, low = halves(x)
    return jnp.concatenate(
        [
            jnp.concatenate([high, high], axis=1),
            jnp.concatenate([low, low], axis=1),
        ],
        axis=0,
    )


def stacked(y):
    high, low = halves(y)
    return jnp.concatenate([high, low], axis=0)


def product(rows, columns):
    both = jnp.dot(rows, columns, preferred_element_type=F32)
    half = both.shape[0] // 2
    return both[:half] + both[half:]


def block_of(ref, k):
    part = ref[pl.ds(k, PAD, stride=LOCAL), :]
    return jnp.concatenate([part, jnp.zeros((PAD, PAD - NODES), F32)], axis=1)


def field_of(ref, k):
    start = k * (2 * NODES)
    return jnp.concatenate(
        [
            ref[pl.ds(start, PAD, stride=2), :],
            ref[pl.ds(start + 1, PAD, stride=2), :],
        ],
        axis=1,
    )


def main_kernel(
    state_h,
    rhs_h,
    modal_ref,
    visc_ref,
    gain_h,
    inv_h,
    rc_h,
    ru_h,
    gl_ref,
    st,
    rh,
    gs,
    iv,
    padm,
    tv,
    vx,
    c,
    sens,
    edge,
    hk,
    hj,
    sm,
    z,
    p4,
    m4,
    zb,
    xb,
    u,
    load_sem,
    hk_send,
    hk_recv,
    hj_send,
    hj_recv,
    c_send,
    c_recv,
    u_send,
    u_recv,
    z_sem,
    x_send,
    x_recv,
    own_sem,
):
    b = lax.axis_index("blk")
    e = lax.axis_index("elem")
    nb = lax.axis_size("blk")
    ne = lax.axis_size("elem")
    bx = b // 2
    bl = b % 2
    rows = 2 * NODES * LOCAL
    pieces = 4
    piece = rows // pieces

    loads = []
    for i in range(pieces):
        part = pl.ds(i * piece, piece)
        loads.append(pltpu.make_async_copy(state_h.at[part], st.at[part], load_sem.at[i]))
    loads.append(pltpu.make_async_copy(rhs_h, rh.at[pl.ds(0, rows)], load_sem.at[4]))
    block_rows = NODES * LOCAL
    loads.append(pltpu.make_async_copy(inv_h, iv.at[pl.ds(0, block_rows)], load_sem.at[5]))
    loads.append(pltpu.make_async_copy(gain_h, gs.at[pl.ds(0, block_rows)], load_sem.at[6]))
    for load in loads:
        load.start()

    barrier = pltpu.get_barrier_semaphore()

    def greet(i, carry):
        pl.semaphore_signal(barrier, inc=1, device_id={"elem": (e + i) % ne}, device_id_type=MESH)
        return carry

    lax.fori_loop(1, ne, greet, 0)
    for d in (1, 2, 4, 6, 7):
        pl.semaphore_signal(barrier, inc=1, device_id={"blk": (b + d) % nb}, device_id_type=MESH)

    st[pl.ds(rows, 8), :] = jnp.zeros((8, PAD), F32)
    rh[pl.ds(rows, 8), :] = jnp.zeros((8, PAD), F32)
    tail = (PAD - NODES) * LOCAL
    gs[pl.ds(block_rows, tail), :] = jnp.zeros((tail, NODES), F32)
    iv[pl.ds(block_rows, tail), :] = jnp.zeros((tail, NODES), F32)

    padm[...] = jnp.zeros((2, PAD, PAD), F32)
    padm[0, 0:NODES, 0:NODES] = modal_ref[...]
    padm[1, 0:NODES, 0:NODES] = visc_ref[...]
    for i in range(2):
        made = as_rows(padm[i])
        tv[pl.ds(i * PAD, PAD), :] = made[:PAD]
        tv[pl.ds((i + 2) * PAD, PAD), :] = made[PAD:]

    def sense(k, carry):
        both = product(tv[...], stacked(field_of(st, k)))
        vx[k] = both[PAD:]
        squares = both[:PAD] * both[:PAD]
        low = jnp.sum(squares[: ORDER**3], axis=0, keepdims=True)
        upper = jnp.sum(squares[ORDER**3 :], axis=0, keepdims=True)
        value = (upper / NODES) / ((low + upper) / NODES + 1e-6)
        sens[0, pl.ds(k, 1), :] = value[:, :PAD]
        sens[1, pl.ds(k, 1), :] = value[:, PAD:]
        return carry

    for i in range(pieces):
        loads[i].wait()
        if i < pieces - 1:
            last = LOCAL // pieces * (i + 1) - 1
            first = LOCAL // pieces * i - (1 if i else 0)
            lax.fori_loop(first, last, sense, 0)
        else:
            lax.fori_loop(LOCAL // pieces * i - 1, LOCAL, sense, 0)

    for j in range(2):
        edge[0, j : j + 1, :] = sens[j, 0:1, :]
        edge[1, j : j + 1, :] = sens[j, LOCAL - 1 : LOCAL, :]
    pl.semaphore_wait(barrier, ne - 1 + 5)

    to_next = pltpu.make_async_remote_copy(
        edge.at[1], hk.at[0], hk_send.at[0], hk_recv.at[0],
        device_id={"blk": (b + 1) % nb}, device_id_type=MESH,
    )
    to_last = pltpu.make_async_remote_copy(
        edge.at[0], hk.at[1], hk_send.at[1], hk_recv.at[1],
        device_id={"blk": (b + nb - 1) % nb}, device_id_type=MESH,
    )
    outer = pltpu.make_async_remote_copy(
        sens.at[1], hj.at[0], hj_send.at[0], hj_recv.at[0],
        device_id={"elem": (e + 1) % ne}, device_id_type=MESH,
    )
    inner = pltpu.make_async_remote_copy(
        sens.at[0], hj.at[1], hj_send.at[1], hj_recv.at[1],
        device_id={"elem": (e + ne - 1) % ne}, device_id_type=MESH,
    )
    for copy in (to_next, to_last, outer, inner):
        copy.start()
    for copy in (to_next, to_last, outer, inner):
        copy.wait()
    has_inner = jnp.where(e > 0, 1.0, 0.0).astype(F32)
    has_outer = jnp.where(e < ne - 1, 1.0, 0.0).astype(F32)
    beside = (hj[0] * has_inner, sens[0], sens[1], hj[1] * has_outer)
    for j in range(2):
        here = sens[j]
        before = jnp.concatenate([hk[0, j : j + 1, :], here[:-1]], axis=0)
        after = jnp.concatenate([here[1:], hk[1, j : j + 1, :]], axis=0)
        sm[j] = (4.0 * here + after + before + beside[j + 2] + beside[j]) / 8.0

    loads[4].wait()
    loads[5].wait()

    def force_one(k):
        scale = jnp.concatenate(
            [
                jnp.broadcast_to(sm[0, pl.ds(k, 1), :], (PAD, PAD)),
                jnp.broadcast_to(sm[1, pl.ds(k, 1), :], (PAD, PAD)),
            ],
            axis=1,
        )
        force = field_of(rh, k) + scale * vx[k]
        coupled = product(as_rows(block_of(iv, k)), stacked(force))
        c[k, 0] = coupled[:, :PAD]
        c[k, 1] = coupled[:, PAD:]

    def early(to):
        return pltpu.make_async_remote_copy(
            c.at[pl.ds(CHUNK * to + 1, CHUNK - 1)], rc_h.at[e], c_send.at[to], c_recv.at[e],
            device_id={"elem": to}, device_id_type=MESH,
        )

    def forcing(i, carry):
        to = (e + i) % ne

        def one(r, inner_carry):
            force_one(CHUNK * to + r)
            return inner_carry

        lax.fori_loop(0, CHUNK, one, 0, unroll=True)
        early(to).start()
        return carry

    lax.fori_loop(1, ne, forcing, 0)
    for r in range(CHUNK):
        force_one(CHUNK * e + r)
    own_c = pltpu.make_async_copy(
        c.at[pl.ds(CHUNK * e + 1, CHUNK - 1)], rc_h.at[e], own_sem.at[0]
    )
    own_c.start()

    loads[6].wait()
    row = lax.broadcasted_iota(jnp.int32, (PAD, PAD), 0)
    column = lax.broadcasted_iota(jnp.int32, (PAD, PAD), 1)
    z[:, pl.ds(0, 2 * PAD)] = jnp.zeros((PAD, 2 * PAD), F32)
    z[:, pl.ds(2 * PAD, PAD)] = jnp.where((row == column) & (row < NODES), 1.0, 0.0).astype(F32)

    def sweep(k):
        made = product(as_rows(block_of(gs, k)), stacked(z[...]))
        z[:, pl.ds(0, PAD)] = made[:, :PAD] + c[k, 0]
        z[:, pl.ds(PAD, PAD)] = made[:, PAD : 2 * PAD] + c[k, 1]
        z[:, pl.ds(2 * PAD, PAD)] = made[:, 2 * PAD :]

    def sweeps(i, carry):
        for r in range(CHUNK):
            sweep(CHUNK * i + r)
            if r == 0:
                p4[i] = z[:, pl.ds(0, 2 * PAD)]
                m4[i] = as_rows(z[:, pl.ds(2 * PAD, PAD)])
        return carry

    lax.fori_loop(0, LOCAL // CHUNK, sweeps, 0)

    zb[bl] = z[...]
    pair = pltpu.make_async_remote_copy(
        zb.at[bl], zb.at[bl], z_sem.at[0], z_sem.at[1],
        device_id={"blk": b + 1 - 2 * bl}, device_id_type=MESH,
    )
    pair.start()
    for i in range(CHUNK - 1):
        gl_ref[i] = as_rows(block_of(gs, CHUNK * e + 1 + i))
    pair.wait()

    def advance(ref, at, field):
        return product(as_rows(ref[at, :, pl.ds(2 * PAD, PAD)]), stacked(field))

    made = advance(zb, 1, zb[0])
    xb[bx, :, pl.ds(0, 2 * PAD)] = made[:, : 2 * PAD] + zb[1, :, pl.ds(0, 2 * PAD)]
    xb[bx, :, pl.ds(2 * PAD, PAD)] = made[:, 2 * PAD :]
    ring = nb // 2

    def along(i):
        return pltpu.make_async_remote_copy(
            xb.at[bx], xb.at[bx], x_send.at[i], x_recv.at[i],
            device_id={"blk": (b + 2 * i) % nb}, device_id_type=MESH,
        )

    for i in range(1, ring):
        along(i).start()
    for i in range(1, ring):
        along(i).wait()

    field = z.at[:, pl.ds(0, 2 * PAD)]
    field[...] = jnp.zeros((PAD, 2 * PAD), F32)

    def pass_pair(i, carry):
        at = i % ring
        field[...] = advance(xb, at, field[...]) + xb[at, :, pl.ds(0, 2 * PAD)]
        return carry

    lax.fori_loop(0, ring + bx, pass_pair, 0)

    @pl.when(bl == 1)
    def _():
        field[...] = advance(zb, 0, field[...]) + zb[0, :, pl.ds(0, 2 * PAD)]

    z_start = m4.at[0]
    start = stacked(field[...])

    def late(to):
        return pltpu.make_async_remote_copy(
            u.at[to], ru_h.at[e], u_send.at[to], u_recv.at[e],
            device_id={"elem": to}, device_id_type=MESH,
        )

    def first_field(to):
        made = product(m4[to], start) + p4[to]
        u[to, 0] = made[:, :PAD]
        u[to, 1] = made[:, PAD:]

    def first_fields(i, carry):
        to = (e + i) % ne
        first_field(to)
        late(to).start()
        return carry

    lax.fori_loop(1, ne, first_fields, 0)
    first_field(e)
    own_u = pltpu.make_async_copy(u.at[e], ru_h.at[e], own_sem.at[1])
    own_u.start()
    own_c.wait()
    own_u.wait()

    def finish(i, carry):
        to = (e + i) % ne
        source = (e + ne - i) % ne
        early(to).wait_send()
        late(to).wait_send()
        pltpu.make_async_remote_copy(
            c.at[pl.ds(CHUNK * to + 1, CHUNK - 1)], rc_h.at[source], c_send.at[to],
            c_recv.at[source], device_id={"elem": to}, device_id_type=MESH,
        ).wait_recv()
        pltpu.make_async_remote_copy(
            u.at[to], ru_h.at[source], u_send.at[to], u_recv.at[source],
            device_id={"elem": to}, device_id_type=MESH,
        ).wait_recv()
        return carry

    lax.fori_loop(1, ne, finish, 0)


def last_kernel(gl_ref, rc_ref, ru_ref, out_ref):
    out = out_ref.reshape(CHUNK * NODES * 8, PAD)
    sources = ru_ref.shape[0]
    pairs = [(s, j) for s in range(sources) for j in range(2)]

    def put(r, field):
        for i in range(len(pairs)):
            out[pl.ds(r * NODES * 8 + i, NODES, stride=8), :] = field[
                :NODES, i * PAD : (i + 1) * PAD
            ]

    field = jnp.concatenate([ru_ref[s, j] for s, j in pairs], axis=1)
    put(0, field)
    for r in range(CHUNK - 1):
        source = jnp.concatenate([rc_ref[s, r, j] for s, j in pairs], axis=1)
        field = product(gl_ref[r], stacked(field)) + source
        put(r + 1, field)


def body(state, rhs, to_modal, viscous_op, sweep_gain, inv_blocks):
    ne = lax.axis_size("elem")
    rows = LOCAL * NODES * 2
    flat = lambda x: x.reshape(rows, PAD)
    blocks = lambda x: jnp.transpose(x, (1, 0, 2)).reshape(NODES * LOCAL, NODES)
    vmem, dma = pltpu.VMEM, pltpu.SemaphoreType.DMA
    anywhere = pl.BlockSpec(memory_space=pl.ANY)
    local = pl.BlockSpec(memory_space=pltpu.VMEM)
    rc, ru, gl = pl.pallas_call(
        main_kernel,
        out_shape=(
            jax.ShapeDtypeStruct((ne, CHUNK - 1, 2, PAD, PAD), F32),
            jax.ShapeDtypeStruct((ne, 2, PAD, PAD), F32),
            jax.ShapeDtypeStruct((CHUNK - 1, 2 * PAD, 2 * PAD), BF16),
        ),
        in_specs=[anywhere, anywhere, local, local, anywhere, anywhere],
        out_specs=(anywhere, anywhere, local),
        scratch_shapes=[
            vmem((rows + 8, PAD), F32),
            vmem((rows + 8, PAD), F32),
            vmem((PAD * LOCAL, NODES), F32),
            vmem((PAD * LOCAL, NODES), F32),
            vmem((2, PAD, PAD), F32),
            vmem((4 * PAD, 2 * PAD), BF16),
            vmem((LOCAL, PAD, 2 * PAD), F32),
            vmem((LOCAL, 2, PAD, PAD), F32),
            vmem((2, LOCAL, PAD), F32),
            vmem((2, 8, PAD), F32),
            vmem((2, 8, PAD), F32),
            vmem((2, LOCAL, PAD), F32),
            vmem((2, LOCAL, PAD), F32),
            vmem((PAD, 3 * PAD), F32),
            vmem((LOCAL // CHUNK, PAD, 2 * PAD), F32),
            vmem((LOCAL // CHUNK, 2 * PAD, 2 * PAD), BF16),
            vmem((2, PAD, 3 * PAD), F32),
            vmem((4, PAD, 3 * PAD), F32),
            vmem((LOCAL // CHUNK, 2, PAD, PAD), F32),
            dma((7,)),
            dma((2,)),
            dma((2,)),
            dma((2,)),
            dma((2,)),
            dma((16,)),
            dma((16,)),
            dma((16,)),
            dma((16,)),
            dma((2,)),
            dma((4,)),
            dma((4,)),
            dma((2,)),
        ],
        compiler_params=pltpu.CompilerParams(
            collective_id=0, has_side_effects=True, vmem_limit_bytes=62 * 2**20
        ),
        name="line_main",
    )(flat(state), flat(rhs), to_modal, viscous_op, blocks(sweep_gain), blocks(inv_blocks))
    out = pl.pallas_call(
        last_kernel,
        grid=(4,),
        out_shape=jax.ShapeDtypeStruct((CHUNK * NODES, 2 * ne, PAD), F32),
        in_specs=[
            pl.BlockSpec((CHUNK - 1, 2 * PAD, 2 * PAD), lambda i: (0, 0, 0)),
            pl.BlockSpec((4, CHUNK - 1, 2, PAD, PAD), lambda i: (i, 0, 0, 0, 0)),
            pl.BlockSpec((4, 2, PAD, PAD), lambda i: (i, 0, 0, 0)),
        ],
        out_specs=pl.BlockSpec((CHUNK * NODES, 8, PAD), lambda i: (0, i, 0)),
        compiler_params=pltpu.CompilerParams(vmem_limit_bytes=48 * 2**20),
        name="line_last",
    )(gl, rc, ru)
    return out.reshape(CHUNK, NODES, 2 * ne, PAD)


def solution(mesh):
    in_specs = (
        P("blk", None, "elem", None),
        P("blk", None, "elem", None),
        P(),
        P(),
        P("blk", None, None),
        P("blk", None, None),
    )
    out_specs = P(("blk", "elem"), None, None, None)
    return jax.shard_map(body, mesh=mesh, in_specs=in_specs, out_specs=out_specs, check_vma=False)
```

time: 599 us -> 177 us (0.30)
  the two profiles are of different devices: /device:TPU:1 before, /device:TPU:109 now
where the time goes in v1:
time: 177 us; the launch traced here: 174 us
  Pallas kernels  172 us (97%)
  local copies, waits for them, and re-layouts  2.58 us (1%)
    pallas_call x1, Pallas kernels, body(): pl.pallas_call(main_kernel, out_shape=(jax.ShapeDtypeStruct((ne, CHUNK -...  164 us
    pallas_call x1, Pallas kernels, body(): pl.pallas_call(last_kernel, grid=(4,), out_shape=jax.ShapeDtypeStruct((CH...  7.86 us

profile of v1, /device:TPU:109, one launch (start us, length us, event | category | flops | bytes accessed | tf_op | source)
XLA Modules:
  0.0 174.2 jit_solution(1864255503741522799)
XLA Ops:
  0.0 163.7 %line_main.1 = (f32[16,3,2,128,128]{4,3,2,1,0:T(8,128)}, f32[16,2,128,128]{3,2,1,0:T(8,128)}, bf16[3,256,256]{2,1,0:T(8,128)(2,1)}) custom-call(f32[16000,128]{1,0:T(8,128)} %bitcast.9, f32[16000,128]{1,0:T(8,128)} %bitcast.10, f32[125,125]{1,0:T(8,128)} %modal_ref.1, f32[125,125]{1,0:T(8,128)} %visc_ref.1, f32[8000,125]{1,0:T(8,128)} %bitcast.11, ...), custom_call_target="tpu_custom_call" | custom-call | tf_op jit(solution)/shard_map/line_main/pallas_call | solution.py:383
  163.7 0.0 copy-start
  163.7 1.6 copy-done
  165.3 0.0 copy-start.1
  165.3 1.0 copy-done.1
  166.3 7.9 %line_last.1 = f32[500,32,128]{2,1,0:T(8,128)} custom-call(bf16[3,256,256]{2,1,0:T(8,128)(2,1)S(1)} %copy-done.1, f32[16,3,2,128,128]{4,3,2,1,0:T(8,128)} %get-tuple-element.9.rc_ref, f32[16,2,128,128]{3,2,1,0:T(8,128)S(1)} %copy-done), custom_call_target="tpu_custom_call" | custom-call | tf_op jit(solution)/shard_map/line_last/pallas_call | solution.py:431
Async XLA Ops:
  163.7 1.6 copy-start
  165.3 1.0 copy-start.1

commit v2 on v1

--- a/solution.py
+++ b/solution.py
@@ -12,6 +12,9 @@
 LOCAL = 64
 CHUNK = 4
 PAD = 128
+PART = 8
+UNROLL = 4
+HOLD = 4
 MESH = pl.DeviceIdType.MESH
 F32 = jnp.float32
 BF16 = jnp.bfloat16
@@ -24,24 +27,16 @@
 
 def as_rows(x):
     high, low = halves(x)
-    return jnp.concatenate(
-        [
-            jnp.concatenate([high, high], axis=1),
-            jnp.concatenate([low, low], axis=1),
-        ],
-        axis=0,
-    )
+    return jnp.concatenate([high, high, low], axis=1)
 
 
 def stacked(y):
     high, low = halves(y)
-    return jnp.concatenate([high, low], axis=0)
+    return jnp.concatenate([high, low, high], axis=0)
 
 
 def product(rows, columns):
-    both = jnp.dot(rows, columns, preferred_element_type=F32)
-    half = both.shape[0] // 2
-    return both[:half] + both[half:]
+    return jnp.dot(rows, columns, preferred_element_type=F32)
 
 
 def block_of(ref, k):
@@ -49,8 +44,7 @@
     return jnp.concatenate([part, jnp.zeros((PAD, PAD - NODES), F32)], axis=1)
 
 
-def field_of(ref, k):
-    start = k * (2 * NODES)
+def field_at(ref, start):
     return jnp.concatenate(
         [
             ref[pl.ds(start, PAD, stride=2), :],
@@ -90,6 +84,8 @@
     xb,
     u,
     load_sem,
+    st_sem,
+    rh_sem,
     hk_send,
     hk_recv,
     hj_send,
@@ -109,20 +105,24 @@
     ne = lax.axis_size("elem")
     bx = b // 2
     bl = b % 2
-    rows = 2 * NODES * LOCAL
-    pieces = 4
-    piece = rows // pieces
-
-    loads = []
-    for i in range(pieces):
-        part = pl.ds(i * piece, piece)
-        loads.append(pltpu.make_async_copy(state_h.at[part], st.at[part], load_sem.at[i]))
-    loads.append(pltpu.make_async_copy(rhs_h, rh.at[pl.ds(0, rows)], load_sem.at[4]))
+    parts = LOCAL // PART
+    part_rows = 2 * NODES * PART
     block_rows = NODES * LOCAL
-    loads.append(pltpu.make_async_copy(inv_h, iv.at[pl.ds(0, block_rows)], load_sem.at[5]))
-    loads.append(pltpu.make_async_copy(gain_h, gs.at[pl.ds(0, block_rows)], load_sem.at[6]))
-    for load in loads:
-        load.start()
+
+    def load_part(source, target, sem, p):
+        first = pl.multiple_of(p * part_rows, 8)
+        return pltpu.make_async_copy(
+            source.at[pl.ds(first, part_rows)], target.at[p, pl.ds(0, part_rows)], sem.at[p]
+        )
+
+    load_inv = pltpu.make_async_copy(inv_h, iv.at[pl.ds(0, block_rows)], load_sem.at[0])
+    load_gain = pltpu.make_async_copy(gain_h, gs.at[pl.ds(0, block_rows)], load_sem.at[1])
+    for p in range(parts):
+        load_part(state_h, st, st_sem, p).start()
+    for p in range(parts):
+        load_part(rhs_h, rh, rh_sem, p).start()
+    load_inv.start()
+    load_gain.start()
 
     barrier = pltpu.get_barrier_semaphore()
 
@@ -134,8 +134,9 @@
     for d in (1, 2, 4, 6, 7):
         pl.semaphore_signal(barrier, inc=1, device_id={"blk": (b + d) % nb}, device_id_type=MESH)
 
-    st[pl.ds(rows, 8), :] = jnp.zeros((8, PAD), F32)
-    rh[pl.ds(rows, 8), :] = jnp.zeros((8, PAD), F32)
+    for p in range(parts):
+        st[p, pl.ds(part_rows, 8), :] = jnp.zeros((8, PAD), F32)
+        rh[p, pl.ds(part_rows, 8), :] = jnp.zeros((8, PAD), F32)
     tail = (PAD - NODES) * LOCAL
     gs[pl.ds(block_rows, tail), :] = jnp.zeros((tail, NODES), F32)
     iv[pl.ds(block_rows, tail), :] = jnp.zeros((tail, NODES), F32)
@@ -144,12 +145,10 @@
     padm[0, 0:NODES, 0:NODES] = modal_ref[...]
     padm[1, 0:NODES, 0:NODES] = visc_ref[...]
     for i in range(2):
-        made = as_rows(padm[i])
-        tv[pl.ds(i * PAD, PAD), :] = made[:PAD]
-        tv[pl.ds((i + 2) * PAD, PAD), :] = made[PAD:]
-
-    def sense(k, carry):
-        both = product(tv[...], stacked(field_of(st, k)))
+        tv[pl.ds(i * PAD, PAD), :] = as_rows(padm[i])
+
+    def sense(source, within, k):
+        both = product(tv[...], stacked(field_at(source, 2 * NODES * within)))
         vx[k] = both[PAD:]
         squares = both[:PAD] * both[:PAD]
         low = jnp.sum(squares[: ORDER**3], axis=0, keepdims=True)
@@ -157,17 +156,19 @@
         value = (upper / NODES) / ((low + upper) / NODES + 1e-6)
         sens[0, pl.ds(k, 1), :] = value[:, :PAD]
         sens[1, pl.ds(k, 1), :] = value[:, PAD:]
-        return carry
-
-    for i in range(pieces):
-        loads[i].wait()
-        if i < pieces - 1:
-            last = LOCAL // pieces * (i + 1) - 1
-            first = LOCAL // pieces * i - (1 if i else 0)
-            lax.fori_loop(first, last, sense, 0)
-        else:
-            lax.fori_loop(LOCAL // pieces * i - 1, LOCAL, sense, 0)
-
+
+    def sense_part(p, carry):
+        load_part(state_h, st, st_sem, p).wait()
+
+        def some(i, inner_carry):
+            for r in range(UNROLL):
+                sense(st.at[p], UNROLL * i + r, PART * p + UNROLL * i + r)
+            return inner_carry
+
+        lax.fori_loop(0, PART // UNROLL, some, 0)
+        return carry
+
+    lax.fori_loop(0, parts, sense_part, 0)
     for j in range(2):
         edge[0, j : j + 1, :] = sens[j, 0:1, :]
         edge[1, j : j + 1, :] = sens[j, LOCAL - 1 : LOCAL, :]
@@ -189,10 +190,10 @@
         sens.at[0], hj.at[1], hj_send.at[1], hj_recv.at[1],
         device_id={"elem": (e + ne - 1) % ne}, device_id_type=MESH,
     )
-    for copy in (to_next, to_last, outer, inner):
+    for copy in (outer, inner, to_next, to_last):
         copy.start()
-    for copy in (to_next, to_last, outer, inner):
-        copy.wait()
+    for copy in (outer, inner, to_next, to_last):
+        copy.wait_recv()
     has_inner = jnp.where(e > 0, 1.0, 0.0).astype(F32)
     has_outer = jnp.where(e < ne - 1, 1.0, 0.0).astype(F32)
     beside = (hj[0] * has_inner, sens[0], sens[1], hj[1] * has_outer)
@@ -202,8 +203,13 @@
         after = jnp.concatenate([here[1:], hk[1, j : j + 1, :]], axis=0)
         sm[j] = (4.0 * here + after + before + beside[j + 2] + beside[j]) / 8.0
 
-    loads[4].wait()
-    loads[5].wait()
+    load_inv.wait()
+
+    def wait_rhs(p, carry):
+        load_part(rhs_h, rh, rh_sem, p).wait()
+        return carry
+
+    lax.fori_loop(0, parts, wait_rhs, 0)
 
     def force_one(k):
         scale = jnp.concatenate(
@@ -213,7 +219,7 @@
             ],
             axis=1,
         )
-        force = field_of(rh, k) + scale * vx[k]
+        force = field_at(rh.at[k // PART], 2 * NODES * (k % PART)) + scale * vx[k]
         coupled = product(as_rows(block_of(iv, k)), stacked(force))
         c[k, 0] = coupled[:, :PAD]
         c[k, 1] = coupled[:, PAD:]
@@ -224,18 +230,42 @@
             device_id={"elem": to}, device_id_type=MESH,
         )
 
-    def forcing(i, carry):
-        to = (e + i) % ne
-
-        def one(r, inner_carry):
+    side = ne // 2
+    mine = side * (e // side)
+
+    def near(d):
+        return mine + (e + d) % side
+
+    def far(d):
+        return side - mine + (e + d) % side
+
+    def forcing(to):
+        for r in range(CHUNK):
             force_one(CHUNK * to + r)
-            return inner_carry
-
-        lax.fori_loop(0, CHUNK, one, 0, unroll=True)
-        early(to).start()
-        return carry
-
-    lax.fori_loop(1, ne, forcing, 0)
+
+    def force_both(d, carry):
+        forcing(far(d))
+        early(far(d)).start()
+        forcing(near(d + 1))
+        early(near(d + 1)).start()
+        return carry
+
+    def force_near(d, carry):
+        forcing(near(d))
+        early(near(d)).start()
+        return carry
+
+    def force_far(d, carry):
+        forcing(far(d))
+        return carry
+
+    def send_far(d, carry):
+        early(far(d)).start()
+        return carry
+
+    lax.fori_loop(0, HOLD, force_both, 0)
+    lax.fori_loop(HOLD + 1, side, force_near, 0)
+    lax.fori_loop(HOLD, side, force_far, 0)
     for r in range(CHUNK):
         force_one(CHUNK * e + r)
     own_c = pltpu.make_async_copy(
@@ -243,7 +273,7 @@
     )
     own_c.start()
 
-    loads[6].wait()
+    load_gain.wait()
     row = lax.broadcasted_iota(jnp.int32, (PAD, PAD), 0)
     column = lax.broadcasted_iota(jnp.int32, (PAD, PAD), 1)
     z[:, pl.ds(0, 2 * PAD)] = jnp.zeros((PAD, 2 * PAD), F32)
@@ -271,6 +301,7 @@
         device_id={"blk": b + 1 - 2 * bl}, device_id_type=MESH,
     )
     pair.start()
+    lax.fori_loop(HOLD, side, send_far, 0)
     for i in range(CHUNK - 1):
         gl_ref[i] = as_rows(block_of(gs, CHUNK * e + 1 + i))
     pair.wait()
@@ -308,7 +339,6 @@
     def _():
         field[...] = advance(zb, 0, field[...]) + zb[0, :, pl.ds(0, 2 * PAD)]
 
-    z_start = m4.at[0]
     start = stacked(field[...])
 
     def late(to):
@@ -334,6 +364,9 @@
     own_u.start()
     own_c.wait()
     own_u.wait()
+
+    for copy in (outer, inner, to_next, to_last):
+        copy.wait_send()
 
     def finish(i, carry):
         to = (e + i) % ne
@@ -375,6 +408,7 @@
 def body(state, rhs, to_modal, viscous_op, sweep_gain, inv_blocks):
     ne = lax.axis_size("elem")
     rows = LOCAL * NODES * 2
+    parts = LOCAL // PART
     flat = lambda x: x.reshape(rows, PAD)
     blocks = lambda x: jnp.transpose(x, (1, 0, 2)).reshape(NODES * LOCAL, NODES)
     vmem, dma = pltpu.VMEM, pltpu.SemaphoreType.DMA
@@ -385,17 +419,17 @@
         out_shape=(
             jax.ShapeDtypeStruct((ne, CHUNK - 1, 2, PAD, PAD), F32),
             jax.ShapeDtypeStruct((ne, 2, PAD, PAD), F32),
-            jax.ShapeDtypeStruct((CHUNK - 1, 2 * PAD, 2 * PAD), BF16),
+            jax.ShapeDtypeStruct((CHUNK - 1, PAD, 3 * PAD), BF16),
         ),
         in_specs=[anywhere, anywhere, local, local, anywhere, anywhere],
         out_specs=(anywhere, anywhere, local),
         scratch_shapes=[
-            vmem((rows + 8, PAD), F32),
-            vmem((rows + 8, PAD), F32),
+            vmem((parts, rows // parts + 8, PAD), F32),
+            vmem((parts, rows // parts + 8, PAD), F32),
             vmem((PAD * LOCAL, NODES), F32),
             vmem((PAD * LOCAL, NODES), F32),
             vmem((2, PAD, PAD), F32),
-            vmem((4 * PAD, 2 * PAD), BF16),
+            vmem((2 * PAD, 3 * PAD), BF16),
             vmem((LOCAL, PAD, 2 * PAD), F32),
             vmem((LOCAL, 2, PAD, PAD), F32),
             vmem((2, LOCAL, PAD), F32),
@@ -405,11 +439,13 @@
             vmem((2, LOCAL, PAD), F32),
             vmem((PAD, 3 * PAD), F32),
             vmem((LOCAL // CHUNK, PAD, 2 * PAD), F32),
-            vmem((LOCAL // CHUNK, 2 * PAD, 2 * PAD), BF16),
+            vmem((LOCAL // CHUNK, PAD, 3 * PAD), BF16),
             vmem((2, PAD, 3 * PAD), F32),
             vmem((4, PAD, 3 * PAD), F32),
             vmem((LOCAL // CHUNK, 2, PAD, PAD), F32),
-            dma((7,)),
+            dma((2,)),
+            dma((parts,)),
+            dma((parts,)),
             dma((2,)),
             dma((2,)),
             dma((2,)),
@@ -433,12 +469,12 @@
         grid=(4,),
         out_shape=jax.ShapeDtypeStruct((CHUNK * NODES, 2 * ne, PAD), F32),
         in_specs=[
-            pl.BlockSpec((CHUNK - 1, 2 * PAD, 2 * PAD), lambda i: (0, 0, 0)),
+            pl.BlockSpec((CHUNK - 1, PAD, 3 * PAD), lambda i: (0, 0, 0)),
             pl.BlockSpec((4, CHUNK - 1, 2, PAD, PAD), lambda i: (i, 0, 0, 0, 0)),
             pl.BlockSpec((4, 2, PAD, PAD), lambda i: (i, 0, 0, 0)),
         ],
         out_specs=pl.BlockSpec((CHUNK * NODES, 8, PAD), lambda i: (0, i, 0)),
-        compiler_params=pltpu.CompilerParams(vmem_limit_bytes=48 * 2**20),
+        compiler_params=pltpu.CompilerParams(vmem_limit_bytes=63 * 2**20),
         name="line_last",
     )(gl, rc, ru)
     return out.reshape(CHUNK, NODES, 2 * ne, PAD)

time: 177 us -> 129 us (0.73); the launches traced: 174 us -> 129 us
  Pallas kernels: 172 us -> 129 us
  local copies, waits for them, and re-layouts: 2.58 us -> 0 us
    pallas_call x1, Pallas kernels: 164 us -> 120 us  [body(): pl.pallas_call(main_kernel, out_shape=(jax.ShapeDtypeStruct((ne, CHUNK -...]
    unnamed x4 -> x0, local copies, waits for them, and re-layouts: 2.58 us -> none
where the time goes in v2:
time: 129 us
  Pallas kernels  129 us (100%)
    pallas_call x1, Pallas kernels, body(): pl.pallas_call(main_kernel, out_shape=(jax.ShapeDtypeStruct((ne, CHUNK -...  120 us
    pallas_call x1, Pallas kernels, body(): pl.pallas_call(last_kernel, grid=(4,), out_shape=jax.ShapeDtypeStruct((CH...  8.54 us

profile of v2, /device:TPU:109, one launch (start us, length us, event | category | flops | bytes accessed | tf_op | source)
XLA Modules:
  0.0 129.0 jit_solution(17887672068792916802)
XLA Ops:
  0.0 120.4 %line_main.1 = (f32[16,3,2,128,128]{4,3,2,1,0:T(8,128)}, f32[16,2,128,128]{3,2,1,0:T(8,128)}, bf16[3,128,384]{2,1,0:T(8,128)(2,1)}) custom-call(f32[16000,128]{1,0:T(8,128)} %bitcast.9, f32[16000,128]{1,0:T(8,128)} %bitcast.10, f32[125,125]{1,0:T(8,128)} %modal_ref.1, f32[125,125]{1,0:T(8,128)} %visc_ref.1, f32[8000,125]{1,0:T(8,128)} %bitcast.11, ...), custom_call_target="tpu_custom_call" | custom-call | tf_op jit(solution)/shard_map/line_main/pallas_call | solution.py:417
  120.4 8.5 %line_last.1 = f32[500,32,128]{2,1,0:T(8,128)} custom-call(bf16[3,128,384]{2,1,0:T(8,128)(2,1)} %get-tuple-element.8.gl_ref, f32[16,3,2,128,128]{4,3,2,1,0:T(8,128)} %get-tuple-element.9.rc_ref, f32[16,2,128,128]{3,2,1,0:T(8,128)} %get-tuple-element.10.ru_ref), custom_call_target="tpu_custom_call" | custom-call | tf_op jit(solution)/shard_map/line_last/pallas_call | solution.py:467

commit v3 on v2

--- a/solution.py
+++ b/solution.py
@@ -12,6 +12,7 @@
 LOCAL = 64
 CHUNK = 4
 PAD = 128
+QUAD = 4
 PART = 8
 UNROLL = 4
 HOLD = 4
@@ -61,7 +62,9 @@
     visc_ref,
     gain_h,
     inv_h,
-    rc_h,
+    rc0_h,
+    rc1_h,
+    rc2_h,
     ru_h,
     gl_ref,
     st,
@@ -70,7 +73,6 @@
     iv,
     padm,
     tv,
-    vx,
     c,
     sens,
     edge,
@@ -149,7 +151,8 @@
 
     def sense(source, within, k):
         both = product(tv[...], stacked(field_at(source, 2 * NODES * within)))
-        vx[k] = both[PAD:]
+        c[k, 0] = both[PAD:, :PAD]
+        c[k, 1] = both[PAD:, PAD:]
         squares = both[:PAD] * both[:PAD]
         low = jnp.sum(squares[: ORDER**3], axis=0, keepdims=True)
         upper = jnp.sum(squares[ORDER**3 :], axis=0, keepdims=True)
@@ -219,16 +222,25 @@
             ],
             axis=1,
         )
-        force = field_at(rh.at[k // PART], 2 * NODES * (k % PART)) + scale * vx[k]
+        force = field_at(rh.at[k // PART], 2 * NODES * (k % PART)) + scale * jnp.concatenate([c[k, 0], c[k, 1]], axis=1)
         coupled = product(as_rows(block_of(iv, k)), stacked(force))
         c[k, 0] = coupled[:, :PAD]
         c[k, 1] = coupled[:, PAD:]
 
+    rc_h = (rc0_h, rc1_h, rc2_h)
+
+    def early_parts(to, source):
+        return [
+            pltpu.make_async_remote_copy(
+                c.at[CHUNK * to + 1 + r], rc_h[r].at[source], c_send.at[r, to],
+                c_recv.at[r, source], device_id={"elem": to}, device_id_type=MESH,
+            )
+            for r in range(CHUNK - 1)
+        ]
+
     def early(to):
-        return pltpu.make_async_remote_copy(
-            c.at[pl.ds(CHUNK * to + 1, CHUNK - 1)], rc_h.at[e], c_send.at[to], c_recv.at[e],
-            device_id={"elem": to}, device_id_type=MESH,
-        )
+        for copy in early_parts(to, e):
+            copy.start()
 
     side = ne // 2
     mine = side * (e // side)
@@ -245,14 +257,14 @@
 
     def force_both(d, carry):
         forcing(far(d))
-        early(far(d)).start()
+        early(far(d))
         forcing(near(d + 1))
-        early(near(d + 1)).start()
+        early(near(d + 1))
         return carry
 
     def force_near(d, carry):
         forcing(near(d))
-        early(near(d)).start()
+        early(near(d))
         return carry
 
     def force_far(d, carry):
@@ -260,7 +272,7 @@
         return carry
 
     def send_far(d, carry):
-        early(far(d)).start()
+        early(far(d))
         return carry
 
     lax.fori_loop(0, HOLD, force_both, 0)
@@ -268,10 +280,12 @@
     lax.fori_loop(HOLD, side, force_far, 0)
     for r in range(CHUNK):
         force_one(CHUNK * e + r)
-    own_c = pltpu.make_async_copy(
-        c.at[pl.ds(CHUNK * e + 1, CHUNK - 1)], rc_h.at[e], own_sem.at[0]
-    )
-    own_c.start()
+    own_c = [
+        pltpu.make_async_copy(c.at[CHUNK * e + 1 + r], rc_h[r].at[e], own_sem.at[1 + r])
+        for r in range(CHUNK - 1)
+    ]
+    for copy in own_c:
+        copy.start()
 
     load_gain.wait()
     row = lax.broadcasted_iota(jnp.int32, (PAD, PAD), 0)
@@ -360,9 +374,10 @@
 
     lax.fori_loop(1, ne, first_fields, 0)
     first_field(e)
-    own_u = pltpu.make_async_copy(u.at[e], ru_h.at[e], own_sem.at[1])
+    own_u = pltpu.make_async_copy(u.at[e], ru_h.at[e], own_sem.at[0])
     own_u.start()
-    own_c.wait()
+    for copy in own_c:
+        copy.wait()
     own_u.wait()
 
     for copy in (outer, inner, to_next, to_last):
@@ -371,12 +386,11 @@
     def finish(i, carry):
         to = (e + i) % ne
         source = (e + ne - i) % ne
-        early(to).wait_send()
         late(to).wait_send()
-        pltpu.make_async_remote_copy(
-            c.at[pl.ds(CHUNK * to + 1, CHUNK - 1)], rc_h.at[source], c_send.at[to],
-            c_recv.at[source], device_id={"elem": to}, device_id_type=MESH,
-        ).wait_recv()
+        for copy in early_parts(to, e):
+            copy.wait_send()
+        for copy in early_parts(to, source):
+            copy.wait_recv()
         pltpu.make_async_remote_copy(
             u.at[to], ru_h.at[source], u_send.at[to], u_recv.at[source],
             device_id={"elem": to}, device_id_type=MESH,
@@ -386,10 +400,10 @@
     lax.fori_loop(1, ne, finish, 0)
 
 
-def last_kernel(gl_ref, rc_ref, ru_ref, out_ref):
+def last_kernel(gl_ref, rc0_ref, rc1_ref, rc2_ref, ru_ref, out_ref):
+    first = QUAD * pl.program_id(0)
     out = out_ref.reshape(CHUNK * NODES * 8, PAD)
-    sources = ru_ref.shape[0]
-    pairs = [(s, j) for s in range(sources) for j in range(2)]
+    pairs = [(s, j) for s in range(QUAD) for j in range(2)]
 
     def put(r, field):
         for i in range(len(pairs)):
@@ -397,10 +411,10 @@
                 :NODES, i * PAD : (i + 1) * PAD
             ]
 
-    field = jnp.concatenate([ru_ref[s, j] for s, j in pairs], axis=1)
+    field = jnp.concatenate([ru_ref[first + s, j] for s, j in pairs], axis=1)
     put(0, field)
-    for r in range(CHUNK - 1):
-        source = jnp.concatenate([rc_ref[s, r, j] for s, j in pairs], axis=1)
+    for r, rc_ref in enumerate((rc0_ref, rc1_ref, rc2_ref)):
+        source = jnp.concatenate([rc_ref[first + s, j] for s, j in pairs], axis=1)
         field = product(gl_ref[r], stacked(field)) + source
         put(r + 1, field)
 
@@ -413,16 +427,20 @@
     blocks = lambda x: jnp.transpose(x, (1, 0, 2)).reshape(NODES * LOCAL, NODES)
     vmem, dma = pltpu.VMEM, pltpu.SemaphoreType.DMA
     anywhere = pl.BlockSpec(memory_space=pl.ANY)
+    far_memory = pl.BlockSpec(memory_space=pltpu.HBM)
     local = pl.BlockSpec(memory_space=pltpu.VMEM)
-    rc, ru, gl = pl.pallas_call(
+    blocks_in = jax.ShapeDtypeStruct((ne, 2, PAD, PAD), F32)
+    rc0, rc1, rc2, ru, gl = pl.pallas_call(
         main_kernel,
         out_shape=(
-            jax.ShapeDtypeStruct((ne, CHUNK - 1, 2, PAD, PAD), F32),
-            jax.ShapeDtypeStruct((ne, 2, PAD, PAD), F32),
+            blocks_in,
+            blocks_in,
+            blocks_in,
+            blocks_in,
             jax.ShapeDtypeStruct((CHUNK - 1, PAD, 3 * PAD), BF16),
         ),
-        in_specs=[anywhere, anywhere, local, local, anywhere, anywhere],
-        out_specs=(anywhere, anywhere, local),
+        in_specs=[far_memory, far_memory, local, local, far_memory, far_memory],
+        out_specs=(anywhere, anywhere, anywhere, anywhere, local),
         scratch_shapes=[
             vmem((parts, rows // parts + 8, PAD), F32),
             vmem((parts, rows // parts + 8, PAD), F32),
@@ -430,7 +448,6 @@
             vmem((PAD * LOCAL, NODES), F32),
             vmem((2, PAD, PAD), F32),
             vmem((2 * PAD, 3 * PAD), BF16),
-            vmem((LOCAL, PAD, 2 * PAD), F32),
             vmem((LOCAL, 2, PAD, PAD), F32),
             vmem((2, LOCAL, PAD), F32),
             vmem((2, 8, PAD), F32),
@@ -450,33 +467,29 @@
             dma((2,)),
             dma((2,)),
             dma((2,)),
-            dma((16,)),
-            dma((16,)),
+            dma((CHUNK - 1, 16)),
+            dma((CHUNK - 1, 16)),
             dma((16,)),
             dma((16,)),
             dma((2,)),
             dma((4,)),
             dma((4,)),
-            dma((2,)),
+            dma((CHUNK,)),
         ],
         compiler_params=pltpu.CompilerParams(
-            collective_id=0, has_side_effects=True, vmem_limit_bytes=62 * 2**20
+            collective_id=0, has_side_effects=True, vmem_limit_bytes=42 * 2**20
         ),
         name="line_main",
     )(flat(state), flat(rhs), to_modal, viscous_op, blocks(sweep_gain), blocks(inv_blocks))
     out = pl.pallas_call(
         last_kernel,
-        grid=(4,),
+        grid=(ne // QUAD,),
         out_shape=jax.ShapeDtypeStruct((CHUNK * NODES, 2 * ne, PAD), F32),
-        in_specs=[
-            pl.BlockSpec((CHUNK - 1, PAD, 3 * PAD), lambda i: (0, 0, 0)),
-            pl.BlockSpec((4, CHUNK - 1, 2, PAD, PAD), lambda i: (i, 0, 0, 0, 0)),
-            pl.BlockSpec((4, 2, PAD, PAD), lambda i: (i, 0, 0, 0)),
-        ],
+        in_specs=[local] * 5,
         out_specs=pl.BlockSpec((CHUNK * NODES, 8, PAD), lambda i: (0, i, 0)),
-        compiler_params=pltpu.CompilerParams(vmem_limit_bytes=63 * 2**20),
+        compiler_params=pltpu.CompilerParams(vmem_limit_bytes=40 * 2**20),
         name="line_last",
-    )(gl, rc, ru)
+    )(gl, rc0, rc1, rc2, ru)
     return out.reshape(CHUNK, NODES, 2 * ne, PAD)
 
 

time: 129 us -> 126 us (0.977)
  Pallas kernels: 129 us -> 125 us
  local copies, waits for them, and re-layouts: 0 us -> 1.68 us
    pallas_call x2, Pallas kernels: 129 us -> 125 us  [the longest x1 119 us: body(): pl.pallas_call(main_kernel, out_shape=(blocks_in, blocks_in, blocks_in, b...]
    unnamed x0 -> x4, local copies, waits for them, and re-layouts: none -> 1.68 us
where the time goes in v3:
time: 126 us
  Pallas kernels  125 us (99%)
  local copies, waits for them, and re-layouts  1.68 us (1%)
    pallas_call x1, Pallas kernels, body(): pl.pallas_call(main_kernel, out_shape=(blocks_in, blocks_in, blocks_in, b...  119 us
    pallas_call x1, Pallas kernels, body(): pl.pallas_call(last_kernel, grid=(ne // QUAD,), out_shape=jax.ShapeDtypeS...  5.24 us

profile of v3, /device:TPU:109, one launch (start us, length us, event | category | flops | bytes accessed | tf_op | source)
XLA Modules:
  0.0 126.2 jit_solution(14684224654689257418)
XLA Ops:
  0.0 0.0 copy-start
  0.0 0.8 copy-done
  0.8 0.0 copy-start.1
  0.8 0.8 copy-done.1
  1.7 119.3 %line_main.1 = (f32[16,2,128,128]{3,2,1,0:T(8,128)S(1)}, f32[16,2,128,128]{3,2,1,0:T(8,128)S(1)}, f32[16,2,128,128]{3,2,1,0:T(8,128)S(1)}, f32[16,2,128,128]{3,2,1,0:T(8,128)S(1)}, bf16[3,128,384]{2,1,0:T(8,128)(2,1)S(1)}) custom-call(f32[16000,128]{1,0:T(8,128)} %bitcast.9, f32[16000,128]{1,0:T(8,128)} %bitcast.10, f32[125,125]{1,0:T(8,128)S(1)} %copy-done, ...), custom_call_target="tpu_custom_call" | custom-call | tf_op jit(solution)/shard_map/line_main/pallas_call | solution.py:433
  121.0 5.2 %line_last.1 = f32[500,32,128]{2,1,0:T(8,128)} custom-call(bf16[3,128,384]{2,1,0:T(8,128)(2,1)S(1)} %get-tuple-element.10.gl_ref, f32[16,2,128,128]{3,2,1,0:T(8,128)S(1)} %get-tuple-element.11.rc0_ref, f32[16,2,128,128]{3,2,1,0:T(8,128)S(1)} %get-tuple-element.12.rc1_ref, f32[16,2,128,128]{3,2,1,0:T(8,128)S(1)} %get-tuple-element.13.rc2_ref, ...), custom_call_target="tpu_custom_call" | custom-call | tf_op jit(solution)/shard_map/line_last/pallas_call | solution.py:484
Async XLA Ops:
  0.0 0.8 copy-start
  0.8 0.8 copy-start.1

commit v4 on v3

--- a/solution.py
+++ b/solution.py
@@ -367,7 +367,7 @@
         u[to, 1] = made[:, PAD:]
 
     def first_fields(i, carry):
-        to = (e + i) % ne
+        to = (e + ne // 2 + i - 1 + (i + ne // 2 - 1) // ne) % ne
         first_field(to)
         late(to).start()
         return carry

time: 126 us -> 128 us (1.016)
  the two profiles are of different devices: /device:TPU:109 before, /device:TPU:21 now
where the time goes in v4:
time: 128 us
  Pallas kernels  126 us (98%)
  local copies, waits for them, and re-layouts  1.68 us (1%)
    pallas_call x1, Pallas kernels, body(): pl.pallas_call(main_kernel, out_shape=(blocks_in, blocks_in, blocks_in, b...  121 us
    pallas_call x1, Pallas kernels, body(): pl.pallas_call(last_kernel, grid=(ne // QUAD,), out_shape=jax.ShapeDtypeS...  5.24 us

profile of v4, /device:TPU:21, one launch (start us, length us, event | category | flops | bytes accessed | tf_op | source)
XLA Modules:
  0.0 127.9 jit_solution(16723324043864263755)
XLA Ops:
  0.0 0.0 copy-start
  0.0 0.8 copy-done
  0.8 0.0 copy-start.1
  0.8 0.8 copy-done.1
  1.7 121.0 %line_main.1 = (f32[16,2,128,128]{3,2,1,0:T(8,128)S(1)}, f32[16,2,128,128]{3,2,1,0:T(8,128)S(1)}, f32[16,2,128,128]{3,2,1,0:T(8,128)S(1)}, f32[16,2,128,128]{3,2,1,0:T(8,128)S(1)}, bf16[3,128,384]{2,1,0:T(8,128)(2,1)S(1)}) custom-call(f32[16000,128]{1,0:T(8,128)} %bitcast.9, f32[16000,128]{1,0:T(8,128)} %bitcast.10, f32[125,125]{1,0:T(8,128)S(1)} %copy-done, ...), custom_call_target="tpu_custom_call" | custom-call | tf_op jit(solution)/shard_map/line_main/pallas_call | solution.py:433
  122.7 5.2 %line_last.1 = f32[500,32,128]{2,1,0:T(8,128)} custom-call(bf16[3,128,384]{2,1,0:T(8,128)(2,1)S(1)} %get-tuple-element.10.gl_ref, f32[16,2,128,128]{3,2,1,0:T(8,128)S(1)} %get-tuple-element.11.rc0_ref, f32[16,2,128,128]{3,2,1,0:T(8,128)S(1)} %get-tuple-element.12.rc1_ref, f32[16,2,128,128]{3,2,1,0:T(8,128)S(1)} %get-tuple-element.13.rc2_ref, ...), custom_call_target="tpu_custom_call" | custom-call | tf_op jit(solution)/shard_map/line_last/pallas_call | solution.py:484
Async XLA Ops:
  0.0 0.8 copy-start
  0.8 0.8 copy-start.1
